TPU v7x, 256 devices: a whole 4x4x8 slice. The times are simulated.
256 devices in a mesh: fsdp: 16 (over z_hi, x, core), dp: 16 (over z_lo, y).
Axes of the slice: x: 4, y: 4, z: 8 (z_hi: 2, z_lo: 4; z = z_hi * 4 + z_lo), core: 2. Of those that a mesh axis runs over, the one named last changes fastest.
Arguments:
- x_pre: bfloat16 [32768, 4096], P(('fsdp', 'dp')), may hold values from -6 to 6
- x_dec: bfloat16 [1024, 4096], P(('fsdp', 'dp')), may hold values from -6 to 6
- rec_hidden: bfloat16 [81920, 4096], P(('fsdp', 'dp')), may hold values from -6 to 6
- norm_gain: bfloat16 [4096], replicated, may hold values from 0.099609375 to 1.8984375
- w_query: bfloat16 [4096, 2048], P(('fsdp', 'dp')), may hold values from -1 to 1
- key_value_weight: bfloat16 [4096, 512], P(('fsdp', 'dp')), may hold values from -0.09375 to 0.09375
- cache_pool: bfloat16 [21504, 64, 512], P(('fsdp', 'dp')), may hold values from -12 to 12
- shared_kv: bfloat16 [131072, 512], P(('fsdp', 'dp')), may hold values from -12 to 12
- dec_len: int32 [256, 4], P(('fsdp', 'dp')), may hold values from 1 to 3072, as said below
- dec_table: int32 [256, 4, 48], P(('fsdp', 'dp')), may hold values from 0 to 83, as said below
- dec_group: int32 [256, 4], P(('fsdp', 'dp')), may hold values from 0 to 15, as said below
- prefix_len: int32 [16, 16], P('fsdp'), may hold values from 1 to 512, as said below
- pre_start: int32 [256], P(('fsdp', 'dp')), may hold values from 0 to 1024, as said below
- pre_table: int32 [256, 16], P(('fsdp', 'dp')), may hold values from 0 to 83, as said below
- rec_req: int32 [256, 320], P(('fsdp', 'dp')), may hold values from 0 to 3, as said below
- rec_off: int32 [256, 320], P(('fsdp', 'dp')), may hold values from 0 to 3071, as said below
Outputs:
- out_pre: bfloat16 [32768, 2048], P(('fsdp', 'dp'))
- out_dec: bfloat16 [1024, 2048], P(('fsdp', 'dp'))
Inputs may be any that keep to these rules, and one draw needn't show every extreme that they name: `dec_len`: the private lengths of one device's decode requests sum to 4096; each device has one request of length exactly 3072. `dec_table`: the pages of one device's decode requests (the first ceil(dec_len / 64) entries of each row) and of its prefill history (the first pre_start / 64 entries) are all different; later entries are valid page numbers. `pre_table`: same pages as stated for dec_table. `dec_group`: A group names a device with the same fsdp index; a few groups along a line are far more common than the others. `prefix_len`: in every fsdp line some device holds a prefix of length exactly 512. `pre_start`: A multiple of 64; some device starts at exactly 1024. `rec_req`: the recomputed tokens of one device are different tokens of its decode requests. `rec_off`: below the request's dec_len.
All inputs are finite; a program needn't handle non-finite values.
Results may differ from a plain program's by a relative error of at most 0.0073.
Values may be sent and summed in bfloat16 or wider, within the bound.
No kernel may reach another device: no remote copies, remote signals or barrier semaphores. Data moves between devices by JAX's collectives and lax.ppermute only.
A program may use at most 192 MiB of HBM per device.

v0:
```python
import jax
import jax.numpy as jnp
from jax import lax
from jax.sharding import PartitionSpec as P

QUERY_HEADS = 16
KEY_VALUE_HEADS = 2
HEAD_SIZE = 128
PAGE_TOKENS = 64
theta_base = 5000000.0
epsilon = 1e-05
negative_large = -1e30


def rms_scaled(values, gain):
    widened = values.astype(jnp.float32)
    factor = lax.rsqrt(jnp.mean(widened * widened, axis=-1, keepdims=True) + epsilon)
    return (widened * factor * gain.astype(jnp.float32)).astype(jnp.bfloat16)


def rotate_halves(vectors, positions):
    half_dim = vectors.shape[-1] // 2
    frequency = theta_base ** (-jnp.arange(half_dim, dtype=jnp.float32) * 2.0 / vectors.shape[-1])
    angles = positions.astype(jnp.float32)[:, None, None] * frequency
    cosines = jnp.cos(angles)
    sines = jnp.sin(angles)
    first_half = vectors[..., :half_dim]
    second_half = vectors[..., half_dim:]
    return jnp.concatenate(
        [first_half * cosines - second_half * sines, second_half * cosines + first_half * sines],
        axis=-1,
    )


def small_lookup(entries, indices):
    matches = indices[..., None] == jnp.arange(entries.shape[0], dtype=jnp.int32)
    return jnp.sum(jnp.where(matches, entries, 0), axis=-1)


def attend_portion(query, keys, values, visible_mask, per_request):
    if per_request:
        score_form = "qojv,qeov->qoje"
        value_form = "wucm,wmuf->wucf"
    else:
        score_form = "rkgd,tkd->rkgt"
        value_form = "rkgt,tkd->rkgd"
    score_matrix = jnp.einsum(
        score_form, query, keys, preferred_element_type=jnp.float32
    ) * query.shape[-1] ** (-0.5)
    allowed = visible_mask[:, None, None, :]
    masked = jnp.where(allowed, score_matrix, negative_large)
    maxima = jnp.max(masked, axis=-1)
    weight_matrix = jnp.where(allowed, jnp.exp(masked - maxima[..., None]), 0.0)
    totals = jnp.sum(weight_matrix, axis=-1)
    summed_output = jnp.einsum(
        value_form, weight_matrix, values.astype(jnp.float32), precision=lax.Precision.HIGHEST
    )
    return (maxima, totals, summed_output)


def combine(first_part, second_part):
    maxima = jnp.maximum(first_part[0], second_part[0])
    left_scale = jnp.exp(first_part[0] - maxima)
    right_scale = jnp.exp(second_part[0] - maxima)
    totals = first_part[1] * left_scale + second_part[1] * right_scale
    summed_output = first_part[2] * left_scale[..., None] + second_part[2] * right_scale[..., None]
    return (maxima, totals, summed_output)


def on_device(
    x_pre,
    x_dec,
    rec_hidden,
    norm_gain,
    w_query,
    key_value_weight,
    cache_pool,
    shared_kv,
    dec_len,
    dec_table,
    dec_group,
    prefix_len,
    pre_start,
    pre_table,
    rec_req,
    rec_off,
):
    group_share = QUERY_HEADS // KEY_VALUE_HEADS
    key_value_width = KEY_VALUE_HEADS * HEAD_SIZE
    prefill_count = x_pre.shape[0]
    decode_count = x_dec.shape[0]
    lengths = dec_len[0]
    page_table = dec_table[0]
    groups = dec_group[0]
    prefix_line = prefix_len[0]
    request = rec_req[0]
    within = rec_off[0]
    query_rows = jnp.concatenate(
        [rms_scaled(x_pre, norm_gain), rms_scaled(x_dec, norm_gain)], axis=0
    )
    key_value_rows = jnp.concatenate([query_rows, rms_scaled(rec_hidden, norm_gain)], axis=0)
    whole_query, whole_keyval = (
        lax.all_gather(w_query, ("fsdp", "dp"), axis=0, tiled=True),
        lax.all_gather(key_value_weight, ("fsdp", "dp"), axis=0, tiled=True),
    )
    query_proj = jnp.dot(query_rows, whole_query, preferred_element_type=jnp.float32)
    key_value_projected = jnp.dot(key_value_rows, whole_keyval, preferred_element_type=jnp.float32)
    pre_pos = pre_start[0] + jnp.arange(prefill_count, dtype=jnp.int32)
    dec_pos = small_lookup(prefix_line, groups) + lengths
    rec_pos = small_lookup(prefix_line, small_lookup(groups, request)) + within
    query_pos = jnp.concatenate([pre_pos, dec_pos], axis=0)
    query_matrix = rotate_halves(query_proj.reshape(-1, QUERY_HEADS, HEAD_SIZE), query_pos).astype(
        jnp.bfloat16
    )
    key_value_positions = jnp.concatenate([query_pos, rec_pos], axis=0)
    key_value_heads = key_value_projected.reshape(-1, 2 * KEY_VALUE_HEADS, HEAD_SIZE)
    new_key_value = jnp.concatenate(
        [
            rotate_halves(key_value_heads[:, :KEY_VALUE_HEADS], key_value_positions),
            key_value_heads[:, KEY_VALUE_HEADS:],
        ],
        axis=1,
    ).astype(jnp.bfloat16)
    added_rows = new_key_value.reshape(-1, 2 * key_value_width)
    max_pages = page_table.shape[1]
    rec_page = page_table.reshape(-1)[request * max_pages + within // PAGE_TOKENS]
    flattened_pool = cache_pool.reshape(-1, 2 * key_value_width)
    flattened_pool = flattened_pool.at[rec_page * PAGE_TOKENS + within % PAGE_TOKENS].set(
        added_rows[prefill_count + decode_count :]
    )
    slot_range = jnp.arange(PAGE_TOKENS, dtype=jnp.int32)
    private_lookup = (page_table[:, :, None] * PAGE_TOKENS + slot_range).reshape(decode_count, -1)
    private_keys = flattened_pool[private_lookup].reshape(
        decode_count, -1, 2 * KEY_VALUE_HEADS, HEAD_SIZE
    )
    private_seen = jnp.arange(private_keys.shape[1], dtype=jnp.int32)[None, :] < lengths[:, None]
    decode_query = query_matrix[prefill_count:].reshape(
        decode_count, KEY_VALUE_HEADS, group_share, HEAD_SIZE
    )
    private_part = attend_portion(
        decode_query,
        private_keys[:, :, :KEY_VALUE_HEADS],
        private_keys[:, :, KEY_VALUE_HEADS:],
        private_seen,
        True,
    )
    fresh_keys = new_key_value[prefill_count : prefill_count + decode_count][:, None]
    fresh_part = attend_portion(
        decode_query,
        fresh_keys[:, :, :KEY_VALUE_HEADS],
        fresh_keys[:, :, KEY_VALUE_HEADS:],
        jnp.ones((decode_count, 1), dtype=bool),
        True,
    )
    local_part = combine(private_part, fresh_part)
    span = shared_kv.shape[0]
    start_portion = (
        jnp.full((decode_count, KEY_VALUE_HEADS, group_share), negative_large, jnp.float32),
        jnp.zeros((decode_count, KEY_VALUE_HEADS, group_share), jnp.float32),
        jnp.zeros((decode_count, KEY_VALUE_HEADS, group_share, HEAD_SIZE), jnp.float32),
    )
    slice_portion = lax.all_gather(shared_kv, "dp", axis=0, tiled=True)
    row_counter = slice_portion.shape[0]
    row_ids = jnp.arange(row_counter, dtype=jnp.int32)
    owner_ids = row_ids // span
    limits = small_lookup(prefix_line, owner_ids)
    visible_mask = (owner_ids[None, :] == groups[:, None]) & (row_ids % span < limits)[None, :]
    head_groups = slice_portion.reshape(row_counter, 2 * KEY_VALUE_HEADS, HEAD_SIZE)
    shared_part = combine(
        start_portion,
        attend_portion(
            decode_query,
            head_groups[:, :KEY_VALUE_HEADS],
            head_groups[:, KEY_VALUE_HEADS:],
            visible_mask,
            False,
        ),
    )
    final_part = combine(local_part, shared_part)
    out_dec = (
        (final_part[2] / final_part[1][..., None])
        .astype(jnp.bfloat16)
        .reshape(decode_count, QUERY_HEADS * HEAD_SIZE)
    )
    history_lookup = (pre_table[0][:, None] * PAGE_TOKENS + slot_range).reshape(-1)
    cached_count = history_lookup.shape[0]
    prefill_context = jnp.concatenate(
        [flattened_pool[history_lookup], added_rows[:prefill_count]], axis=0
    ).reshape(-1, 2 * KEY_VALUE_HEADS, HEAD_SIZE)
    row_ids = jnp.arange(prefill_count, dtype=jnp.int32)
    pre_visible = jnp.concatenate(
        [
            jnp.broadcast_to(
                jnp.arange(cached_count, dtype=jnp.int32)[None, :] < pre_start[0],
                (prefill_count, cached_count),
            ),
            row_ids[None, :] <= row_ids[:, None],
        ],
        axis=1,
    )
    prefill_query = query_matrix[:prefill_count].reshape(
        prefill_count, KEY_VALUE_HEADS, group_share, HEAD_SIZE
    )
    prefill_scores = jnp.einsum(
        "uwvm,owm->wvuo",
        prefill_query,
        prefill_context[:, :KEY_VALUE_HEADS],
        preferred_element_type=jnp.float32,
    ) * HEAD_SIZE ** (-0.5)
    pre_allowed = pre_visible[None, None]
    pre_masked = jnp.where(pre_allowed, prefill_scores, negative_large)
    pre_max = jnp.max(pre_masked, axis=-1, keepdims=True)
    pre_weights = jnp.where(pre_allowed, jnp.exp(pre_masked - pre_max), 0.0)
    prefill_probabilities = (pre_weights / jnp.sum(pre_weights, axis=-1, keepdims=True)).astype(
        jnp.bfloat16
    )
    out_pre = jnp.einsum(
        "jcse,eji->sjci",
        prefill_probabilities,
        prefill_context[:, KEY_VALUE_HEADS:],
        preferred_element_type=jnp.float32,
    )
    return (out_pre.astype(jnp.bfloat16).reshape(prefill_count, QUERY_HEADS * HEAD_SIZE), out_dec)


def solution(mesh):
    return jax.shard_map(
        on_device,
        mesh=mesh,
        in_specs=(
            P(("fsdp", "dp"), None),
            P(("fsdp", "dp"), None),
            P(("fsdp", "dp"), None),
            P(),
            P(("fsdp", "dp"), None),
            P(("fsdp", "dp"), None),
            P(("fsdp", "dp"), None, None),
            P(("fsdp", "dp"), None),
            P(("fsdp", "dp"), None),
            P(("fsdp", "dp"), None, None),
            P(("fsdp", "dp"), None),
            P("fsdp", None),
            P(("fsdp", "dp")),
            P(("fsdp", "dp"), None),
            P(("fsdp", "dp"), None),
            P(("fsdp", "dp"), None),
        ),
        out_specs=(P(("fsdp", "dp"), None), P(("fsdp", "dp"), None)),
        check_vma=False,
    )
```

profile of v0, /device:TPU:1, one launch (start us, length us, event | category | flops | bytes accessed | tf_op | source)
XLA Modules:
  0.0 1581.3 jit_solution(894209553763811438)
XLA Ops:
  7.3 5.7 copy.216
  13.9 1.0 copy.125
  16.5 2.4 gather_fusion
  20.3 1.6 fusion.28
  25.5 1.3 fusion.30
  26.8 2.3 fusion.10
  29.2 695.2 %all-gather.4.cloned.1.call-done = bf16[4096,512]{1,0:T(8,128)(2,1)} async-done(((bf16[16,512]{1,0:T(8,128)(2,1)}), bf16[4096,512]{1,0:T(8,128)(2,1)}) %all-gather.4.cloned.1.call-update) | async-done | bytes 4194320 | tf_op jit(solution)/shard_map/all_gather | solution.py:104
  724.4 5.4 fusion.16
  733.1 7.9 scatter_custom_fusion
  741.1 7.3 gather_fusion.1
  748.9 1.3 copy.118
  750.2 53.4 %gather_fusion.2 = bf16[12288,512]{1,0:T(8,128)(2,1)} fusion(bf16[5376,512]{1,0:T(8,128)(2,1)} %scatter_custom_fusion, s32[12288]{0:T(1024)S(1)} %broadcast_clamp_fusion), kind=kCustom, calls=%fused_computation.2 | custom fusion | bytes 25214976 | tf_op jit(solution)/shard_map/gather | solution.py:133
  803.6 18.2 %reshape.645 = bf16[4,3072,4,128]{3,2,1,0:T(4,128)(2,1)} reshape(bf16[12288,512]{1,0:T(8,128)(2,1)} %gather_fusion.2) | data formatting | bytes 25165824 | tf_op jit(solution)/shard_map/reshape | solution.py:133
  821.9 16.0 %fusion.127 = (bf16[4,3072,2,128]{3,2,1,0:T(2,128)(2,1)}, bf16[4,3072,2,128]{3,2,1,0:T(2,128)(2,1)}) fusion(bf16[4,3072,4,128]{3,2,1,0:T(4,128)(2,1)} %reshape.645), kind=kLoop, calls=%fused_computation.182 | loop fusion | bytes 25165824 | tf_op jit(solution)/shard_map/slice | solution.py:143
  838.0 618.8 %all-gather.6.cloned.1.call-done = bf16[4096,2048]{1,0:T(8,128)(2,1)} async-done(((bf16[16,2048]{1,0:T(8,128)(2,1)}), bf16[4096,2048]{1,0:T(8,128)(2,1)}) %all-gather.6.cloned.1.call-update) | async-done | bytes 16777232 | tf_op jit(solution)/shard_map/all_gather | solution.py:103
  1456.7 8.2 fusion.35
  1466.5 6.5 fusion.128
  1472.9 4.7 fusion.34
  1477.6 1.0 copy.133
  1478.8 81.8 %all-gather.8.cloned.1.call-done = bf16[8192,512]{0,1:T(8,128)(2,1)} async-done(((bf16[512,512]{0,1:T(8,128)(2,1)}), bf16[8192,512]{0,1:T(8,128)(2,1)}) %all-gather.8.cloned.1.call-update) | async-done | bytes 8388624 | tf_op jit(solution)/shard_map/all_gather | solution.py:162
  1560.6 3.3 fusion.131
  1564.7 1.8 fusion.132
  1567.4 4.0 fusion.48
  1571.4 2.7 fusion.69
  (122 shorter events, 14.3 us)
Async XLA Ops:
  7.2 8.7 copy-start.11
  7.2 8.7 copy-start.8
  7.2 6.7 copy-start.5
  7.2 9.2 copy-start.17
  7.2 7.9 copy-start.12
  7.2 8.8 copy-start.15
  7.2 8.8 copy-start.14
  7.2 12.3 copy-start.18
  7.2 7.7 copy-start.13
  7.3 7.7 copy-start.10
  7.3 717.1 %all-gather.4.cloned.1.call-start = ((), (), s32[]{:S(2)}) async-start(), calls=%async_computation | async-start | bytes 4210688 | tf_op jit(solution)/shard_map/all_gather | solution.py:104
  13.1 8.8 copy-start
  13.1 1443.7 %all-gather.6.cloned.1.call-start = ((), (), s32[]{:S(2)}) async-start(), calls=%async_computation.1 | async-start | bytes 16842752 | tf_op jit(solution)/shard_map/all_gather | solution.py:103
  13.8 1546.8 %all-gather.8.cloned.1.call-start = ((), (), s32[]{:S(2)}) async-start(), calls=%async_computation.2 | async-start | bytes 8912896 | tf_op jit(solution)/shard_map/all_gather | solution.py:162
  20.2 5.3 copy-start.2
  22.5 6.6 copy-start.16
  821.9 634.8 %copy-start.1 = (bf16[128,4096]{1,0:T(8,128)(2,1)S(1)}, bf16[128,4096]{1,0:T(8,128)(2,1)}, u32[]{:S(2)}) copy-start(bf16[128,4096]{1,0:T(8,128)(2,1)} %fusion.30) | copy-start | bytes 3145732
  1465.2 1.2 copy-start.7
  1478.6 86.1 %slice-start = ((s8[6291456]{0:T(1024)(128)(4,1)}), s8[2097152]{0:T(1024)(128)(4,1)S(1)}, s32[]{:S(2)}) async-start(s8[6291456]{0:T(1024)(128)(4,1)} %bitcast.130), calls=%async_computation.3 | async-start | bytes 4194304
  1560.6 4.0 slice-start.1
  1560.6 4.0 copy-start.9
  1563.9 3.4 copy-start.3
  1564.7 6.7 slice-start.2
  1566.9 4.6 slice-start.3
  (2 other events, 2.4 us)
Sparse Core Ops, SparseCore 0:
  13.2 711.1 all-gather.3
  726.2 730.4 all-gather.5
  1458.5 102.0 all-gather.7
where the time goes:
time: 1580 us
  waiting for transfers between devices  1400 us (89%)
  local copies, waits for them, and re-layouts  118 us (7%)
  matrix products  36.7 us (2%)
    all_gather x1, waiting for transfers between devices, on_device(): lax.all_gather(key_value_weight, ('fsdp', 'dp'), axis=0, tiled=True)  695 us
    all_gather x1, waiting for transfers between devices, on_device(): lax.all_gather(w_query, ('fsdp', 'dp'), axis=0, tiled=True)  619 us
    all_gather x1, waiting for transfers between devices, on_device(): slice_portion = lax.all_gather(shared_kv, 'dp', axis=0, tiled=True)  81.8 us
    gather x1, local copies, waits for them, and re-layouts, on_device(): flattened_pool[private_lookup]  53.4 us
  transfers between devices with their start and end apart: 3, of which 3 were waited for; matrix products, arithmetic and copies ran while one was open for 9% of the time, Pallas kernels for 0%

commit v1 on v0

--- a/solution.py
+++ b/solution.py
@@ -99,9 +99,18 @@
         [rms_scaled(x_pre, norm_gain), rms_scaled(x_dec, norm_gain)], axis=0
     )
     key_value_rows = jnp.concatenate([query_rows, rms_scaled(rec_hidden, norm_gain)], axis=0)
+    fit_array = lambda a0: jnp.concatenate(
+        lax.all_to_all(
+            jnp.stack([a0] * lax.psum(1, axis_name=("fsdp", "dp"))),
+            axis_name=("fsdp", "dp"),
+            split_axis=0,
+            concat_axis=0,
+        ),
+        axis=0,
+    )
     whole_query, whole_keyval = (
         lax.all_gather(w_query, ("fsdp", "dp"), axis=0, tiled=True),
-        lax.all_gather(key_value_weight, ("fsdp", "dp"), axis=0, tiled=True),
+        fit_array(key_value_weight),
     )
     query_proj = jnp.dot(query_rows, whole_query, preferred_element_type=jnp.float32)
     key_value_projected = jnp.dot(key_value_rows, whole_keyval, preferred_element_type=jnp.float32)

time: 1580 us -> 905 us (0.57)
  waiting for transfers between devices: 1400 us -> 689 us
  starting transfers between devices: 0.12 us -> 16.7 us
    all_gather x1 -> x0, waiting for transfers between devices: 695 us -> none  [on_device(): lax.all_gather(key_value_weight, ('fsdp', 'dp'), axis=0, tiled=True)]
    all_gather x1, waiting for transfers between devices: 619 us -> 518 us  [on_device(): lax.all_gather(w_query, ('fsdp', 'dp'), axis=0, tiled=True)]
    all_to_all x0 -> x1, waiting for transfers between devices: none -> 85.9 us  [on_device(): lax.all_to_all(jnp.stack([a0] * lax.psum(1, axis_name=('fsdp', 'dp'))), a...]
    all_to_all x0 -> x1, starting transfers between devices: none -> 16.7 us  [on_device(): lax.all_to_all(jnp.stack([a0] * lax.psum(1, axis_name=('fsdp', 'dp'))), a...]
  transfers between devices with their start and end apart: 3 -> 3, of which waited for: 3 -> 3; matrix products, arithmetic and copies ran while one was open for 9% -> 18% of each run, Pallas kernels for 0% -> 0%
where the time goes in v1:
time: 905 us; the launch traced here: 903 us
  waiting for transfers between devices  689 us (76%)
  local copies, waits for them, and re-layouts  130 us (14%)
  matrix products  36.1 us (4%)
  starting transfers between devices  16.7 us (2%)
  between operations  15.3 us (2%)
  other arithmetic  15.2 us (2%)
    all_gather x1, waiting for transfers between devices, on_device(): lax.all_gather(w_query, ('fsdp', 'dp'), axis=0, tiled=True)  518 us
    all_to_all x1, waiting for transfers between devices, on_device(): lax.all_to_all(jnp.stack([a0] * lax.psum(1, axis_name=('fsdp', 'dp'))), a...  85.9 us
    all_gather x1, waiting for transfers between devices, on_device(): slice_portion = lax.all_gather(shared_kv, 'dp', axis=0, tiled=True)  85.4 us
    gather x1, local copies, waits for them, and re-layouts, on_device(): flattened_pool[private_lookup]  57.3 us
    reshape x1, local copies, waits for them, and re-layouts, on_device(): flattened_pool[private_lookup]  18.2 us
  transfers between devices with their start and end apart: 3, of which 3 were waited for; matrix products, arithmetic and copies ran while one was open for 18% of the time, Pallas kernels for 0%

profile of v1, /device:TPU:1, one launch (start us, length us, event | category | flops | bytes accessed | tf_op | source)
XLA Modules:
  0.0 902.7 jit_solution(5248746416793368621)
XLA Ops:
  7.2 5.6 copy.189
  12.9 2.6 stack.2
  15.6 16.7 %all-to-all-start = ((bf16[256,16,512]{2,1,0:T(8,128)(2,1)}), bf16[256,16,512]{2,1,0:T(8,128)(2,1)}, u32[]{:S(2)}, u32[]{:S(2)}) async-start(bf16[256,16,512]{2,1,0:T(8,128)(2,1)} %stack.2), calls=%async_computation | async-start | bytes 8388608 | tf_op jit(solution)/shard_map/all_to_all | solution.py:103
  34.5 1.5 fusion.27
  36.5 2.4 gather_fusion
  44.5 1.3 fusion.29
  45.8 2.3 fusion.10
  48.3 85.9 %all-to-all-done = bf16[256,16,512]{2,1,0:T(8,128)(2,1)} async-done(((bf16[256,16,512]{2,1,0:T(8,128)(2,1)}), bf16[256,16,512]{2,1,0:T(8,128)(2,1)}, u32[]{:S(2)}, u32[]{:S(2)}) %all-to-all-start) | async-done | bytes 4194336 | tf_op jit(solution)/shard_map/all_to_all | solution.py:103
  134.1 6.5 copy.88
  140.7 5.1 fusion.16
  146.8 7.9 scatter_custom_fusion
  154.8 7.3 gather_fusion.1
  163.3 57.3 %gather_fusion.2 = bf16[12288,512]{1,0:T(8,128)(2,1)} fusion(bf16[5376,512]{1,0:T(8,128)(2,1)} %scatter_custom_fusion, s32[12288]{0:T(1024)} %broadcast_clamp_fusion), kind=kCustom, calls=%fused_computation.2 | custom fusion | bytes 25214976 | tf_op jit(solution)/shard_map/gather | solution.py:142
  220.6 18.2 %reshape.649 = bf16[4,3072,4,128]{3,2,1,0:T(4,128)(2,1)} reshape(bf16[12288,512]{1,0:T(8,128)(2,1)} %gather_fusion.2) | data formatting | bytes 25165824 | tf_op jit(solution)/shard_map/reshape | solution.py:142
  240.6 16.0 %fusion.114 = (bf16[4,3072,2,128]{3,2,1,0:T(2,128)(2,1)}, bf16[4,3072,2,128]{3,2,1,0:T(2,128)(2,1)}) fusion(bf16[4,3072,4,128]{3,2,1,0:T(4,128)(2,1)} %reshape.649), kind=kLoop, calls=%fused_computation.178 | loop fusion | bytes 25165824 | tf_op jit(solution)/shard_map/slice | solution.py:152
  256.7 518.0 %all-gather.3.cloned.1.call-done = bf16[4096,2048]{1,0:T(8,128)(2,1)} async-done(((bf16[16,2048]{1,0:T(8,128)(2,1)}), bf16[4096,2048]{1,0:T(8,128)(2,1)}) %all-gather.3.cloned.1.call-update) | async-done | bytes 16777232 | tf_op jit(solution)/shard_map/all_gather | solution.py:112
  774.6 8.2 fusion.35
  784.3 6.1 fusion.115
  790.4 4.7 fusion.33
  796.3 85.4 %all-gather.5.cloned.1.call-done = bf16[8192,512]{0,1:T(8,128)(2,1)} async-done(((bf16[512,512]{0,1:T(8,128)(2,1)}), bf16[8192,512]{0,1:T(8,128)(2,1)}) %all-gather.5.cloned.1.call-update) | async-done | bytes 8388624 | tf_op jit(solution)/shard_map/all_gather | solution.py:171
  881.7 3.3 fusion.116
  885.8 1.8 fusion.117
  888.4 4.1 fusion.48
  892.5 2.7 fusion.69
  (134 shorter events, 16.3 us)
Async XLA Ops:
  7.2 5.7 copy-start.15
  7.2 767.5 %all-gather.3.cloned.1.call-start = ((), (), s32[]{:S(2)}) async-start(), calls=%async_computation.1 | async-start | bytes 16842752 | tf_op jit(solution)/shard_map/all_gather | solution.py:112
  15.5 16.8 %copy-start.9 = (bf16[512,512]{1,0:T(8,128)(2,1)S(1)}, bf16[512,512]{1,0:T(8,128)(2,1)}, u32[]{:S(2)}) copy-start(bf16[512,512]{1,0:T(8,128)(2,1)} %param.23) | copy-start | bytes 1572868
  15.5 17.9 %copy-start.19 = (s32[1,320]{1,0:T(1,128)S(1)}, s32[1,320]{1,0:T(1,128)}, u32[]{:S(2)}) copy-start(s32[1,320]{1,0:T(1,128)} %param.30) | copy-start | bytes 3844
  15.5 17.9 %copy-start.16 = (s32[1,320]{1,0:T(1,128)S(1)}, s32[1,320]{1,0:T(1,128)}, u32[]{:S(2)}) copy-start(s32[1,320]{1,0:T(1,128)} %param.31) | copy-start | bytes 3844
  15.5 18.0 %copy-start.18 = (s32[1,4,48]{2,1,0:T(4,128)S(1)}, s32[1,4,48]{2,1,0:T(4,128)}, u32[]{:S(2)}) copy-start(s32[1,4,48]{2,1,0:T(4,128)} %param.25) | copy-start | bytes 2308
  15.5 18.7 %copy-start.13 = (bf16[4,4096]{1,0:T(4,128)(2,1)S(1)}, bf16[4,4096]{1,0:T(4,128)(2,1)}, u32[]{:S(2)}) copy-start(bf16[4,4096]{1,0:T(4,128)(2,1)} %param.17) | copy-start | bytes 98308
  15.6 20.4 %copy-start.20 = (s32[1,16]{1,0:T(1,128)S(1)}, s32[1,16]{1,0:T(1,128)}, u32[]{:S(2)}) copy-start(s32[1,16]{1,0:T(1,128)} %param.27) | copy-start | bytes 196
  15.6 20.4 %copy-start.21 = (s32[1,4]{1,0:T(1,128)S(1)}, s32[1,4]{1,0:T(1,128)}, u32[]{:S(2)}) copy-start(s32[1,4]{1,0:T(1,128)} %param.26) | copy-start | bytes 52
  15.6 20.8 %copy-start.23 = (s32[1,4]{1,0:T(1,128)S(1)}, s32[1,4]{1,0:T(1,128)}, u32[]{:S(2)}) copy-start(s32[1,4]{1,0:T(1,128)} %param.24) | copy-start | bytes 52
  15.6 118.6 %all-to-all-start = ((bf16[256,16,512]{2,1,0:T(8,128)(2,1)}), bf16[256,16,512]{2,1,0:T(8,128)(2,1)}, u32[]{:S(2)}, u32[]{:S(2)}) async-start(bf16[256,16,512]{2,1,0:T(8,128)(2,1)} %stack.2), calls=%async_computation | async-start | bytes 8388608 | tf_op jit(solution)/shard_map/all_to_all | solution.py:103
  32.3 7.3 copy-start.24
  32.3 7.7 copy-start.17
  32.3 8.0 copy-start
  32.3 849.4 %all-gather.5.cloned.1.call-start = ((), (), s32[]{:S(2)}) async-start(), calls=%async_computation.2 | async-start | bytes 8912896 | tf_op jit(solution)/shard_map/all_gather | solution.py:171
  44.5 96.2 %copy-start.11 = (bf16[4,4096]{1,0:T(4,128)(2,1)}, bf16[4,4096]{1,0:T(4,128)(2,1)S(1)}, u32[]{:S(2)}) copy-start(bf16[4,4096]{1,0:T(4,128)(2,1)S(1)} %fusion.83) | copy-start | bytes 98308
  134.1 6.6 copy-start.1
  220.6 18.2 %copy-start.4 = (bf16[452,2,64]{2,0,1:T(8,128)(2,1)S(1)}, bf16[452,2,64]{2,0,1:T(8,128)(2,1)}, u32[]{:S(2)}) copy-start(bf16[452,2,64]{2,0,1:T(8,128)(2,1)} %copy-done.3) | copy-start | bytes 347140
  220.6 18.2 %copy-start.6 = (bf16[452,2,128]{2,0,1:T(8,128)(2,1)S(1)}, bf16[452,2,128]{2,0,1:T(8,128)(2,1)}, u32[]{:S(2)}) copy-start(bf16[452,2,128]{2,0,1:T(8,128)(2,1)} %copy-done.5) | copy-start | bytes 694276
  240.6 534.0 %copy-start.12 = (bf16[4,4096]{1,0:T(4,128)(2,1)S(1)}, bf16[4,4096]{1,0:T(4,128)(2,1)}, u32[]{:S(2)}) copy-start(bf16[4,4096]{1,0:T(4,128)(2,1)} %copy-done.11) | copy-start | bytes 98308
  790.4 5.8 copy-start.22
  796.1 89.6 %slice-start = ((s8[6291456]{0:T(1024)(128)(4,1)}), s8[2097152]{0:T(1024)(128)(4,1)S(1)}, s32[]{:S(2)}) async-start(s8[6291456]{0:T(1024)(128)(4,1)} %bitcast.138), calls=%async_computation.3 | async-start | bytes 4194304
  885.8 6.7 slice-start.2
  887.9 4.6 slice-start.3
  (8 other events, 19.8 us)
Sparse Core Ops, SparseCore 0:
  13.0 761.5 all-gather.2
  776.4 105.2 all-gather.4
